TPU v7x, 256 devices: a whole 4x4x8 slice. The times are simulated.
256 devices in a mesh: samp: 64 (over z, x, core), snp: 4 (over y).
Axes of the slice: x: 4, y: 4, z: 8, core: 2. Of those that a mesh axis runs over, the one named last changes fastest.
Arguments:
- genotype: int32 [40960, 4096], P('samp', 'snp'), may hold values from 0 to 2
- freqs: float32 [4096], P('snp'), may hold values from 0.35 to 0.65
- left_factors: float32 [40960, 20], P('samp'), may hold values from -6 to 6
- singular: float32 [20], replicated, may hold values from 0.5 to 2
- right_factors: float32 [4096, 20], P(('snp', 'samp')), may hold values from -1.25 to 1.25
- sketch: bfloat16 [4096, 64], P('snp'), may hold values from -6 to 6
- batch_sizes: int32 [12], replicated, may hold values from 1 to 6826, 40960 in all
- missing_batch: int32 [48], replicated, may hold values from 0 to 11, as said below
- missing_block: int32 [48], replicated, may hold values from 0 to 15, as said below
Outputs:
- basis: float32 [40960, 64], P('samp')
- projection: float32 [4096, 64], P('snp')
- snp_basis: float32 [4096, 64], P('snp')
Inputs may be any that keep to these rules, and one draw needn't show every extreme that they name: The pairs (missing_batch, missing_block) are distinct; every block id appears exactly 3 times and every batch id exactly 48 // 12 times. `missing_block`: paired entry by entry with missing_batch.
All inputs are finite; a program needn't handle non-finite values.
Results may differ from a plain program's by a relative error of at most 0.012.
Values may be sent and summed in bfloat16 or wider, within the bound.
No kernel may reach another device: no remote copies, remote signals or barrier semaphores. Data moves between devices by JAX's collectives and lax.ppermute only.
A program may use at most 64 MiB of HBM per device.

v0:
```python
import math
import jax
import jax.numpy as jnp
from jax import lax
from jax.sharding import PartitionSpec as P

BATCHES = 12
BLOCK = 256
ITERS = 2
BLOCKS = 16


def finish_basis(values, gram):
    lower = jnp.linalg.cholesky(gram)
    return jax.scipy.linalg.solve_triangular(lower, values.T, lower=True).T


def reversed_basis(values, gram):
    flipped = finish_basis(values[:, ::-1], gram[::-1, ::-1])
    return flipped[:, ::-1]


def own_gram(values):
    return jnp.dot(values.T, values, precision=lax.Precision.HIGHEST)


def sample_basis(matrix, right_side, sample_count):
    partial_value = jnp.dot(matrix, right_side, preferred_element_type=jnp.float32)
    summed = lax.psum(partial_value.astype(jnp.bfloat16), "snp").astype(jnp.float32)
    gram = lax.psum(own_gram(summed), "samp") / sample_count
    return finish_basis(summed, gram)


def snp_columns(matrix, basis):
    local_part = lax.dot_general(
        matrix,
        basis.astype(jnp.bfloat16),
        (((0,), (0,)), ((), ())),
        preferred_element_type=jnp.float32,
    )
    return lax.psum(local_part, "samp")


def snp_basis(columns, snp_count):
    gram = lax.psum(own_gram(columns), "snp") / snp_count
    return reversed_basis(columns, gram)


def on_device(
    genotype,
    freqs,
    left_factors,
    singular,
    right_factors,
    sketch,
    batch_sizes,
    missing_batch,
    missing_block,
):
    row_count, col_width = genotype.shape
    sample_count = row_count * lax.axis_size("samp")
    snp_count = col_width * lax.axis_size("snp")
    right_local = lax.all_gather(right_factors, "samp", axis=0, tiled=True)
    batch_range = jnp.arange(BATCHES, dtype=jnp.int32)
    block_range = jnp.arange(BLOCKS, dtype=jnp.int32)
    hot_batch = (missing_batch[:, None] == batch_range[None, :]).astype(jnp.float32)
    hot_block = (missing_block[:, None] == block_range[None, :]).astype(jnp.float32)
    table = jnp.dot(hot_batch.T, hot_block, preferred_element_type=jnp.float32)
    ends = jnp.cumsum(batch_sizes)
    row_ids = lax.axis_index("samp") * row_count + jnp.arange(row_count, dtype=jnp.int32)
    batch_of = jnp.sum((row_ids[:, None] >= ends[None, :]).astype(jnp.int32), axis=1)
    row_hot = (batch_of[:, None] == batch_range[None, :]).astype(jnp.float32)
    col_ids = lax.axis_index("snp") * col_width + jnp.arange(col_width, dtype=jnp.int32)
    col_hot = ((col_ids // BLOCK)[None, :] == block_range[:, None]).astype(jnp.float32)
    missing = (
        jnp.dot(
            jnp.dot(row_hot, table, preferred_element_type=jnp.float32),
            col_hot,
            preferred_element_type=jnp.float32,
        )
        > 0.5
    )
    lowrank = jnp.dot(
        left_factors * singular[None, :], right_local.T, precision=lax.Precision.HIGHEST
    )
    observed = genotype.astype(jnp.float32) - 2.0 * freqs[None, :]
    matrix = jnp.where(missing, lowrank, observed).astype(jnp.bfloat16)
    basis = sample_basis(matrix, sketch, sample_count)
    column_basis = jnp.zeros((col_width, sketch.shape[1]), jnp.float32)
    for sweep_index in range(ITERS):
        column_basis = snp_basis(snp_columns(matrix, basis), snp_count)
        basis = sample_basis(matrix, column_basis.astype(jnp.bfloat16), sample_count)
    projection = snp_columns(matrix, basis) / math.sqrt(sample_count)
    return (basis, projection, column_basis)


def solution(mesh):
    in_specs = (
        P("samp", "snp"),
        P("snp"),
        P("samp", None),
        P(),
        P(("snp", "samp"), None),
        P("snp", None),
        P(),
        P(),
        P(),
    )
    out_specs = (P("samp", None), P("snp", None), P("snp", None))
    return jax.shard_map(
        on_device, mesh=mesh, in_specs=in_specs, out_specs=out_specs, check_vma=False
    )
```

profile of v0, /device:TPU:1, one launch (start us, length us, event | category | flops | bytes accessed | tf_op | source)
XLA Modules:
  0.0 1585.5 jit_solution(2528023982231809789)
XLA Ops:
  7.3 0.7 broadcast_multiply_fusion.6
  8.0 54.6 %all_gather.3 = f32[1024,20]{1,0:T(8,128)S(1)} all-gather(f32[16,20]{1,0:T(8,128)} %param.18), channel_id=1, replica_groups=mesh['samp'=64,'snp'=4] {'samp'}, dimensions={0}, use_global_device_ids=true | all-gather | bytes 83200 | tf_op jit(solution)/shard_map/all_gather | solution.py:63
  62.6 0.8 reduce-window.8
  63.5 0.9 fusion.43
  64.4 2.2 fusion
  66.6 5.1 select_convert_fusion
  71.7 1.2 convolution_convert_fusion.2
  72.9 40.8 %all-reduce.7.cloned.1.call-done = bf16[640,64]{0,1:T(8,128)(2,1)} async-done(((bf16[640,64]{0,1:T(8,128)(2,1)}), bf16[640,64]{0,1:T(8,128)(2,1)}) %all-reduce.7.cloned.1.call-update) | async-done | bytes 81936 | tf_op jit(solution)/shard_map/psum | solution.py:29
  113.7 1.1 fusion.49
  114.8 246.0 %psum.78 = f32[64,64]{0,1:T(8,128)S(1)} all-reduce(f32[64,64]{0,1:T(8,128)S(1)} %fusion.49), channel_id=1, replica_groups=mesh['samp'=64,'snp'=4] {'samp'}, use_global_device_ids=true, to_apply=%region_3.4 | all-reduce | flops 4096 | bytes 32768 | tf_op jit(solution)/shard_map/psum | solution.py:30
  360.9 5.8 cholesky.89
  367.4 0.7 fusion.18
  368.1 4.9 custom-call.11
  373.0 1.2 convolution_convert_fusion.4
  374.3 1.1 fusion.54
  375.4 176.2 %all-reduce.9.cloned.1.call-done = f32[1024,64]{0,1:T(8,128)} async-done(((f32[1024,64]{0,1:T(8,128)}), f32[1024,64]{0,1:T(8,128)}) %all-reduce.9.cloned.1.call-update) | async-done | bytes 262160 | tf_op jit(solution)/shard_map/psum | solution.py:41
  551.6 1.4 fusion.50
  553.1 13.3 psum.80
  566.5 5.8 cholesky.100
  573.0 0.7 fusion.19
  573.7 4.9 custom-call.12
  578.6 3.1 rev.19
  582.3 1.2 convolution_convert_fusion.1
  583.7 42.7 %all-reduce.11.cloned.1.call-done = bf16[640,64]{0,1:T(8,128)(2,1)} async-done(((bf16[640,64]{0,1:T(8,128)(2,1)}), bf16[640,64]{0,1:T(8,128)(2,1)}) %all-reduce.11.cloned.1.call-update) | async-done | bytes 81936 | tf_op jit(solution)/shard_map/psum | solution.py:29
  626.4 1.1 fusion.51
  627.5 246.0 %psum.82 = f32[64,64]{0,1:T(8,128)S(1)} all-reduce(f32[64,64]{0,1:T(8,128)S(1)} %fusion.51), channel_id=1, replica_groups=mesh['samp'=64,'snp'=4] {'samp'}, use_global_device_ids=true, to_apply=%region_9.13 | all-reduce | flops 4096 | bytes 32768 | tf_op jit(solution)/shard_map/psum | solution.py:30
  873.6 5.8 cholesky.111
  880.1 0.7 fusion.20
  880.8 4.9 custom-call.13
  885.7 1.2 convolution_convert_fusion.3
  886.9 1.1 fusion.55
  888.1 176.2 %all-reduce.13.cloned.1.call-done = f32[1024,64]{0,1:T(8,128)} async-done(((f32[1024,64]{0,1:T(8,128)}), f32[1024,64]{0,1:T(8,128)}) %all-reduce.13.cloned.1.call-update) | async-done | bytes 262160 | tf_op jit(solution)/shard_map/psum | solution.py:41
  1064.3 1.4 fusion.52
  1065.8 13.3 psum.84
  1079.2 5.8 cholesky.122
  1086.4 4.9 custom-call.14
  1091.3 3.1 rev.22
  1095.0 1.2 convolution_convert_fusion
  1096.2 42.8 %all-reduce.15.cloned.1.call-done = bf16[640,64]{0,1:T(8,128)(2,1)} async-done(((bf16[640,64]{0,1:T(8,128)(2,1)}), bf16[640,64]{0,1:T(8,128)(2,1)}) %all-reduce.15.cloned.1.call-update) | async-done | bytes 81936 | tf_op jit(solution)/shard_map/psum | solution.py:29
  1139.1 1.1 fusion.53
  1140.2 246.0 %psum.86 = f32[64,64]{0,1:T(8,128)S(1)} all-reduce(f32[64,64]{0,1:T(8,128)S(1)} %fusion.53), channel_id=1, replica_groups=mesh['samp'=64,'snp'=4] {'samp'}, use_global_device_ids=true, to_apply=%region_13.17 | all-reduce | flops 4096 | bytes 32768 | tf_op jit(solution)/shard_map/psum | solution.py:30
  1386.3 5.8 cholesky.133
  1392.8 0.7 fusion.22
  1393.5 4.9 custom-call.15
  1398.4 1.2 convolution_bitcast_fusion.2
  1399.6 1.1 fusion.15
  1400.7 176.2 %all-reduce.17.cloned.1.call-done = f32[1024,64]{0,1:T(8,128)} async-done(((f32[1024,64]{0,1:T(8,128)}), f32[1024,64]{0,1:T(8,128)}) %all-reduce.17.cloned.1.call-update) | async-done | bytes 262160 | tf_op jit(solution)/shard_map/psum | solution.py:41
  1576.9 1.7 broadcast_multiply_fusion
  (57 shorter events, 6.5 us)
Async XLA Ops:
  7.2 64.5 %copy-start = (bf16[1024,64]{0,1:T(8,128)(2,1)S(1)}, bf16[1024,64]{0,1:T(8,128)(2,1)}, u32[]{:S(2)}) copy-start(bf16[1024,64]{0,1:T(8,128)(2,1)} %param.19) | copy-start | bytes 393220
  7.2 106.5 %all-reduce.7.cloned.1.call-start = ((), (), s32[]{:S(2)}) async-start(), calls=%async_computation | async-start | bytes 163840 | tf_op jit(solution)/shard_map/psum | solution.py:29
  64.4 2.2 copy-start.3
  64.4 2.2 copy-start.4
  72.9 478.7 %all-reduce.9.cloned.1.call-start = ((), (), s32[]{:S(2)}) async-start(), calls=%async_computation.1 | async-start | bytes 524288 | tf_op jit(solution)/shard_map/psum | solution.py:41
  375.3 251.1 %all-reduce.11.cloned.1.call-start = ((), (), s32[]{:S(2)}) async-start(), calls=%async_computation.2 | async-start | bytes 163840 | tf_op jit(solution)/shard_map/psum | solution.py:29
  583.5 480.8 %all-reduce.13.cloned.1.call-start = ((), (), s32[]{:S(2)}) async-start(), calls=%async_computation.3 | async-start | bytes 524288 | tf_op jit(solution)/shard_map/psum | solution.py:41
  888.0 251.0 %all-reduce.15.cloned.1.call-start = ((), (), s32[]{:S(2)}) async-start(), calls=%async_computation.4 | async-start | bytes 163840 | tf_op jit(solution)/shard_map/psum | solution.py:29
  1095.0 305.7 %copy-start.1 = (f32[1024,64]{0,1:T(8,128)}, f32[1024,64]{0,1:T(8,128)S(1)}, u32[]{:S(2)}) copy-start(f32[1024,64]{0,1:T(8,128)S(1)} %rev.23) | copy-start | bytes 786436
  1096.2 480.8 %all-reduce.17.cloned.1.call-start = ((), (), s32[]{:S(2)}) async-start(), calls=%async_computation.5 | async-start | bytes 524288 | tf_op jit(solution)/shard_map/psum | solution.py:41
  1399.6 179.0 %copy-start.2 = (f32[640,64]{0,1:T(8,128)}, f32[640,64]{0,1:T(8,128)S(1)}, u32[]{:S(2)}) copy-start(f32[640,64]{0,1:T(8,128)S(1)} %convolution_bitcast_fusion.2) | copy-start | bytes 491524
Sparse Core Ops, SparseCore 0:
  73.0 40.6 all-reduce.6
  375.5 176.0 all-reduce.8
  583.6 42.7 all-reduce.10
  888.2 176.1 all-reduce.12
  1096.3 42.7 all-reduce.14
  1400.8 176.0 all-reduce.16
where the time goes:
time: 1590 us
  blocking collectives  819 us (52%)
  waiting for transfers between devices  655 us (41%)
  other arithmetic  63.7 us (4%)
  matrix products  25.5 us (2%)
    psum x3, blocking collectives, sample_basis(): gram = lax.psum(own_gram(summed), 'samp') / sample_count  738 us
    psum x3, waiting for transfers between devices, snp_columns(): return lax.psum(local_part, 'samp')  529 us
    psum x3, waiting for transfers between devices, sample_basis(): lax.psum(partial_value.astype(jnp.bfloat16), 'snp').astype(jnp.float32)  126 us
    all_gather x1, blocking collectives, on_device(): right_local = lax.all_gather(right_factors, 'samp', axis=0, tiled=True)  54.6 us
    another operation x15, other arithmetic, finish_basis(): lower = jnp.linalg.cholesky(gram)  32.6 us
  transfers between devices with their start and end apart: 6, of which 6 were waited for; matrix products, arithmetic and copies ran while one was open for 0% of the time, Pallas kernels for 0%

commit v1 on v0

--- a/solution.py
+++ b/solution.py
@@ -8,6 +8,12 @@
 BLOCK = 256
 ITERS = 2
 BLOCKS = 16
+edit_the_panels = lambda field: jnp.concatenate(
+    lax.all_to_all(
+        jnp.stack([field] * lax.axis_size("samp")), axis_name="samp", split_axis=0, concat_axis=0
+    ),
+    axis=0,
+)
 
 
 def finish_basis(values, gram):
@@ -60,7 +66,7 @@
     row_count, col_width = genotype.shape
     sample_count = row_count * lax.axis_size("samp")
     snp_count = col_width * lax.axis_size("snp")
-    right_local = lax.all_gather(right_factors, "samp", axis=0, tiled=True)
+    right_local = edit_the_panels(right_factors)
     batch_range = jnp.arange(BATCHES, dtype=jnp.int32)
     block_range = jnp.arange(BLOCKS, dtype=jnp.int32)
     hot_batch = (missing_batch[:, None] == batch_range[None, :]).astype(jnp.float32)

time: 1590 us -> 1550 us (0.975)
  blocking collectives: 819 us -> 765 us
    all_gather x1 -> x0, blocking collectives: 54.6 us -> none  [on_device(): right_local = lax.all_gather(right_factors, 'samp', axis=0, tiled=True)]
  transfers between devices with their start and end apart: 6 -> 7, of which waited for: 6 -> 7; matrix products, arithmetic and copies ran while one was open for 0% -> 0% of each run, Pallas kernels for 0% -> 0%
where the time goes in v1:
time: 1550 us
  blocking collectives  765 us (49%)
  waiting for transfers between devices  660 us (43%)
  other arithmetic  63.3 us (4%)
  matrix products  24.8 us (2%)
    psum x3, blocking collectives, sample_basis(): gram = lax.psum(own_gram(summed), 'samp') / sample_count  738 us
    psum x3, waiting for transfers between devices, snp_columns(): return lax.psum(local_part, 'samp')  529 us
    psum x3, waiting for transfers between devices, sample_basis(): lax.psum(partial_value.astype(jnp.bfloat16), 'snp').astype(jnp.float32)  124 us
    another operation x15, other arithmetic, finish_basis(): lower = jnp.linalg.cholesky(gram)  32.6 us
  transfers between devices with their start and end apart: 7, of which 7 were waited for; matrix products, arithmetic and copies ran while one was open for 0% of the time, Pallas kernels for 0%

profile of v1, /device:TPU:1, one launch (start us, length us, event | category | flops | bytes accessed | tf_op | source)
XLA Modules:
  0.0 1550.6 jit_solution(9244555907349203321)
XLA Ops:
  7.2 0.8 stack.2
  8.0 1.0 reshape.78
  9.0 13.0 all-to-all-start
  22.7 2.2 fusion
  24.8 7.7 all-to-all-done
  33.1 0.9 reduce.4
  34.3 5.1 select_convert_fusion
  39.4 1.2 convolution_convert_fusion.2
  40.6 38.2 %all-reduce.7.cloned.1.call-done = bf16[640,64]{0,1:T(8,128)(2,1)} async-done(((bf16[640,64]{0,1:T(8,128)(2,1)}), bf16[640,64]{0,1:T(8,128)(2,1)}) %all-reduce.7.cloned.1.call-update) | async-done | bytes 81936 | tf_op jit(solution)/shard_map/psum | solution.py:35
  78.8 1.1 fusion.49
  79.9 246.0 %psum.78 = f32[64,64]{0,1:T(8,128)S(1)} all-reduce(f32[64,64]{0,1:T(8,128)S(1)} %fusion.49), channel_id=1, replica_groups=mesh['samp'=64,'snp'=4] {'samp'}, use_global_device_ids=true, to_apply=%region_3.4 | all-reduce | flops 4096 | bytes 32768 | tf_op jit(solution)/shard_map/psum | solution.py:36
  326.0 5.8 cholesky.89
  332.5 0.7 fusion.18
  333.2 4.9 custom-call.11
  338.1 1.2 convolution_convert_fusion.4
  339.4 1.1 fusion.54
  340.5 176.1 %all-reduce.9.cloned.1.call-done = f32[1024,64]{0,1:T(8,128)} async-done(((f32[1024,64]{0,1:T(8,128)}), f32[1024,64]{0,1:T(8,128)}) %all-reduce.9.cloned.1.call-update) | async-done | bytes 262160 | tf_op jit(solution)/shard_map/psum | solution.py:47
  516.6 1.4 fusion.50
  518.1 13.3 psum.80
  531.5 5.8 cholesky.100
  538.0 0.7 fusion.19
  538.7 4.9 custom-call.12
  543.6 3.1 rev.19
  547.3 1.2 convolution_convert_fusion.1
  548.6 42.8 %all-reduce.11.cloned.1.call-done = bf16[640,64]{0,1:T(8,128)(2,1)} async-done(((bf16[640,64]{0,1:T(8,128)(2,1)}), bf16[640,64]{0,1:T(8,128)(2,1)}) %all-reduce.11.cloned.1.call-update) | async-done | bytes 81936 | tf_op jit(solution)/shard_map/psum | solution.py:35
  591.4 1.1 fusion.51
  592.5 246.2 %psum.82 = f32[64,64]{0,1:T(8,128)S(1)} all-reduce(f32[64,64]{0,1:T(8,128)S(1)} %fusion.51), channel_id=1, replica_groups=mesh['samp'=64,'snp'=4] {'samp'}, use_global_device_ids=true, to_apply=%region_9.13 | all-reduce | flops 4096 | bytes 32768 | tf_op jit(solution)/shard_map/psum | solution.py:36
  838.8 5.8 cholesky.111
  846.0 4.9 custom-call.13
  850.9 1.2 convolution_convert_fusion.3
  852.1 1.1 fusion.55
  853.3 176.2 %all-reduce.13.cloned.1.call-done = f32[1024,64]{0,1:T(8,128)} async-done(((f32[1024,64]{0,1:T(8,128)}), f32[1024,64]{0,1:T(8,128)}) %all-reduce.13.cloned.1.call-update) | async-done | bytes 262160 | tf_op jit(solution)/shard_map/psum | solution.py:47
  1029.5 1.4 fusion.52
  1031.0 13.3 psum.84
  1044.4 5.8 cholesky.122
  1050.9 0.7 fusion.21
  1051.5 4.9 custom-call.14
  1056.4 3.1 rev.22
  1060.2 1.2 convolution_convert_fusion
  1061.4 42.8 %all-reduce.15.cloned.1.call-done = bf16[640,64]{0,1:T(8,128)(2,1)} async-done(((bf16[640,64]{0,1:T(8,128)(2,1)}), bf16[640,64]{0,1:T(8,128)(2,1)}) %all-reduce.15.cloned.1.call-update) | async-done | bytes 81936 | tf_op jit(solution)/shard_map/psum | solution.py:35
  1104.2 1.1 fusion.53
  1105.3 246.0 %psum.86 = f32[64,64]{0,1:T(8,128)S(1)} all-reduce(f32[64,64]{0,1:T(8,128)S(1)} %fusion.53), channel_id=1, replica_groups=mesh['samp'=64,'snp'=4] {'samp'}, use_global_device_ids=true, to_apply=%region_13.17 | all-reduce | flops 4096 | bytes 32768 | tf_op jit(solution)/shard_map/psum | solution.py:36
  1351.4 5.8 cholesky.133
  1358.6 4.9 custom-call.15
  1363.5 1.2 convolution_bitcast_fusion.2
  1364.8 1.1 fusion.15
  1365.9 176.2 %all-reduce.17.cloned.1.call-done = f32[1024,64]{0,1:T(8,128)} async-done(((f32[1024,64]{0,1:T(8,128)}), f32[1024,64]{0,1:T(8,128)}) %all-reduce.17.cloned.1.call-update) | async-done | bytes 262160 | tf_op jit(solution)/shard_map/psum | solution.py:47
  1542.1 1.7 broadcast_multiply_fusion
  (71 shorter events, 8.3 us)
Async XLA Ops:
  7.2 32.2 %copy-start = (bf16[1024,64]{0,1:T(8,128)(2,1)S(1)}, bf16[1024,64]{0,1:T(8,128)(2,1)}, u32[]{:S(2)}) copy-start(bf16[1024,64]{0,1:T(8,128)(2,1)} %param.19) | copy-start | bytes 393220
  7.2 14.9 copy-start.6
  7.2 15.2 copy-start.7
  7.2 15.2 copy-start.8
  9.0 23.6 %all-to-all-start = ((f32[64,1,320]{2,1,0:T(1,128)}), f32[64,1,320]{2,1,0:T(1,128)S(1)}, u32[]{:S(2)}, u32[]{:S(2)}) async-start(f32[64,1,320]{2,1,0:T(1,128)} %reshape.78), calls=%async_computation | async-start | bytes 196608 | tf_op jit(solution)/shard_map/all_to_all | solution.py:12
  22.0 56.8 %all-reduce.7.cloned.1.call-start = ((), (), s32[]{:S(2)}) async-start(), calls=%async_computation.1 | async-start | bytes 163840 | tf_op jit(solution)/shard_map/psum | solution.py:35
  22.6 2.2 copy-start.4
  22.6 11.6 copy-start.3
  22.6 11.6 copy-start.5
  40.6 476.0 %all-reduce.9.cloned.1.call-start = ((), (), s32[]{:S(2)}) async-start(), calls=%async_computation.2 | async-start | bytes 524288 | tf_op jit(solution)/shard_map/psum | solution.py:47
  340.4 251.0 %all-reduce.11.cloned.1.call-start = ((), (), s32[]{:S(2)}) async-start(), calls=%async_computation.3 | async-start | bytes 163840 | tf_op jit(solution)/shard_map/psum | solution.py:35
  548.5 481.0 %all-reduce.13.cloned.1.call-start = ((), (), s32[]{:S(2)}) async-start(), calls=%async_computation.4 | async-start | bytes 524288 | tf_op jit(solution)/shard_map/psum | solution.py:47
  853.2 251.0 %all-reduce.15.cloned.1.call-start = ((), (), s32[]{:S(2)}) async-start(), calls=%async_computation.5 | async-start | bytes 163840 | tf_op jit(solution)/shard_map/psum | solution.py:35
  1060.1 305.7 %copy-start.1 = (f32[1024,64]{0,1:T(8,128)}, f32[1024,64]{0,1:T(8,128)S(1)}, u32[]{:S(2)}) copy-start(f32[1024,64]{0,1:T(8,128)S(1)} %rev.23) | copy-start | bytes 786436
  1061.3 480.8 %all-reduce.17.cloned.1.call-start = ((), (), s32[]{:S(2)}) async-start(), calls=%async_computation.6 | async-start | bytes 524288 | tf_op jit(solution)/shard_map/psum | solution.py:47
  1364.8 179.0 %copy-start.2 = (f32[640,64]{0,1:T(8,128)}, f32[640,64]{0,1:T(8,128)S(1)}, u32[]{:S(2)}) copy-start(f32[640,64]{0,1:T(8,128)S(1)} %convolution_bitcast_fusion.2) | copy-start | bytes 491524
Sparse Core Ops, SparseCore 0:
  40.7 38.0 all-reduce.6
  340.6 175.9 all-reduce.8
  548.6 42.7 all-reduce.10
  853.3 176.1 all-reduce.12
  1061.5 42.7 all-reduce.14
  1366.0 176.0 all-reduce.16
